TPU v7x, 32 devices: a whole 2x2x4 slice. The times are simulated.
32 devices in a mesh: fsdp: 8 (over z, x), rep: 4 (over y, core).
Axes of the slice: x: 2, y: 2, z: 4, core: 2. Of those that a mesh axis runs over, the one named last changes fastest.
Arguments:
- tokens_x: bfloat16 [4096, 8192], P(('fsdp', 'rep')), may hold values from -6 to 6
- cotangent: bfloat16 [4096, 128], P(('fsdp', 'rep')), may hold values from -1 to 1
- master_weight: float32 [8192, 128], P('fsdp'), may hold values from -0.015625 to 0.015625
- first_moment: float32 [8192, 128], P('fsdp'), may hold values from -6 to 6
- second_moment: float32 [8192, 128], P('fsdp'), may hold values from 0.5 to 2
- hidden_dec: bfloat16 [2, 64, 8192], P(None, ('fsdp', 'rep')), may hold values from -6 to 6
- queries: bfloat16 [2, 64, 1024], P(None, ('fsdp', 'rep')), may hold values from -64 to 64
- new_values: bfloat16 [2, 64, 128], P(None, ('fsdp', 'rep')), may hold values from -6 to 6
- key_cache: bfloat16 [64, 1024, 128], P(('fsdp', 'rep')), may hold values from -64 to 64
- value_cache: bfloat16 [64, 1024, 128], P(('fsdp', 'rep')), may hold values from -6 to 6
- cache_lengths: int32 [64], P(('fsdp', 'rep')), may hold values from 2 to 1022, as said below
Outputs:
- weight_next: float32 [8192, 128], P('fsdp')
- first_next: float32 [8192, 128], P('fsdp')
- second_next: float32 [8192, 128], P('fsdp')
- rollout_weight: bfloat16 [8192, 128], replicated
- fresh_keys: bfloat16 [2, 64, 128], P(None, ('fsdp', 'rep'))
- attended: bfloat16 [2, 64, 1024], P(None, ('fsdp', 'rep'))
Inputs may be any that keep to these rules, and one draw needn't show every extreme that they name: `cache_lengths`: some row has exactly 1022 filled slots.
All inputs are finite; a program needn't handle non-finite values. Where the computation divides by a largest or mean magnitude, that divisor is 1e-20 or more.
Results may differ from a plain program's by a relative error of at most 0.0049.
Values may be sent and summed in bfloat16 or wider, within the bound.
A program may use at most 64 MiB of HBM per device.

v0:
```python
import math
import jax
import jax.numpy as jnp
from jax import lax
from jax.sharding import PartitionSpec as P

D = 8192
BLOCK = 128
beta_one = 0.9
beta_two = 0.95
adam_eps = 1e-08
learn_rate = 0.0003
weight_decay = 0.1
step_count = 100
rope_theta = 1000000.0
peak_eps = 1e-06


def adamw(weight, first, second, gradient):
    first_new = beta_one * first + (1.0 - beta_one) * gradient
    second_new = beta_two * second + (1.0 - beta_two) * gradient * gradient
    first_hat = first_new / (1.0 - beta_one**step_count)
    second_hat = second_new / (1.0 - beta_two**step_count)
    weight_new = weight - learn_rate * (
        first_hat / (jnp.sqrt(second_hat) + adam_eps) + weight_decay * weight
    )
    return (weight_new, first_new, second_new)


def rotate(values, positions):
    half = values.shape[-1] // 2
    freq = rope_theta ** (-jnp.arange(half, dtype=jnp.float32) * 2.0 / values.shape[-1])
    angle = positions.astype(jnp.float32)[..., None] * freq
    cosine = jnp.cos(angle)
    sine = jnp.sin(angle)
    first_half = values[..., :half]
    second_half = values[..., half:]
    return jnp.concatenate(
        [first_half * cosine - second_half * sine, second_half * cosine + first_half * sine],
        axis=-1,
    )


def project_keys(hidden_size, quantized_weight, scales, lengths):
    decode_step_count, row_count, block_width = hidden_size.shape
    block_count = scales.shape[0]
    part_count = jnp.einsum(
        "qht,hti->qhi",
        hidden_size.reshape(decode_step_count * row_count, block_count, block_width // block_count),
        quantized_weight.reshape(block_count, block_width // block_count, -1),
        preferred_element_type=jnp.float32,
    )
    raw = jnp.sum(part_count * scales[None, :, None], axis=1).reshape(
        decode_step_count, row_count, -1
    )
    positions = lengths[None, :] + jnp.arange(decode_step_count, dtype=jnp.int32)[:, None]
    return rotate(raw, positions).astype(jnp.bfloat16)


def attend(query, cache_keys, cache_values, fresh, fresh_values, lengths):
    decode_step_count, row_count, joined = query.shape
    head_dim = cache_keys.shape[-1]
    heads = joined // head_dim
    valid = jnp.arange(cache_keys.shape[1], dtype=jnp.int32)[None, None, :] < lengths[:, None, None]
    outputs = []
    for section_index in range(decode_step_count):
        query_now = query[section_index].reshape(row_count, heads, head_dim)
        scores_c = jnp.einsum(
            "rhd,rcd->rhc", query_now, cache_keys, preferred_element_type=jnp.float32
        ) / math.sqrt(head_dim)
        scores_f = jnp.einsum(
            "rhd,trd->rht", query_now, fresh, preferred_element_type=jnp.float32
        ) / math.sqrt(head_dim)
        scores_c = jnp.where(valid, scores_c, -jnp.inf)
        scores_f = jnp.where(
            (jnp.arange(decode_step_count) <= section_index)[None, None, :], scores_f, -jnp.inf
        )
        peak = jnp.maximum(jnp.max(scores_c, axis=2), jnp.max(scores_f, axis=2))[:, :, None]
        exp_c = jnp.exp(scores_c - peak)
        exp_f = jnp.exp(scores_f - peak)
        total = jnp.sum(exp_c, axis=2, keepdims=True) + jnp.sum(exp_f, axis=2, keepdims=True)
        prob_c = (exp_c / total).astype(jnp.bfloat16)
        prob_f = (exp_f / total).astype(jnp.bfloat16)
        mixed = jnp.einsum("rhc,rcd->rhd", prob_c, cache_values, preferred_element_type=jnp.float32)
        mixed = mixed + jnp.einsum(
            "rht,trd->rhd", prob_f, fresh_values, preferred_element_type=jnp.float32
        )
        outputs.append(mixed.reshape(row_count, joined).astype(jnp.bfloat16))
    return jnp.stack(outputs)


def shards(
    tokens_x,
    cotangent,
    master_weight,
    first_moment,
    second_moment,
    hidden_dec,
    queries,
    new_values,
    key_cache,
    value_cache,
    cache_lengths,
):
    shard_rows = master_weight.shape[0]
    partial_grad = lax.psum_scatter(
        lax.dot_general(
            tokens_x, cotangent, (((0,), (0,)), ((), ())), preferred_element_type=jnp.float32
        ),
        "fsdp",
        scatter_dimension=0,
        tiled=True,
    )
    gradient = lax.psum(partial_grad, "rep")
    weight_next, first_next, second_next = adamw(
        master_weight, first_moment, second_moment, gradient
    )
    block_count = D // BLOCK
    row_ids = lax.axis_index("fsdp") * shard_rows + jnp.arange(shard_rows, dtype=jnp.int32)
    member = (row_ids // BLOCK)[:, None] == jnp.arange(block_count, dtype=jnp.int32)[None, :]
    row_peak = jnp.max(jnp.abs(weight_next), axis=1)
    local_peaks = jnp.max(jnp.where(member, row_peak[:, None], 0.0), axis=0)
    scales = lax.pmax(local_peaks, "fsdp") + peak_eps
    row_scale = jnp.sum(jnp.where(member, scales[None, :], 0.0), axis=1)
    local_quant = (weight_next / row_scale[:, None]).astype(jnp.bfloat16)
    rollout_weight = lax.all_gather(local_quant, "fsdp", axis=0, tiled=True)
    fresh_keys = project_keys(hidden_dec, rollout_weight, scales, cache_lengths)
    attended = attend(queries, key_cache, value_cache, fresh_keys, new_values, cache_lengths)
    return (weight_next, first_next, second_next, rollout_weight, fresh_keys, attended)


def solution(mesh):
    return jax.shard_map(
        shards,
        mesh=mesh,
        in_specs=(
            P(("fsdp", "rep"), None),
            P(("fsdp", "rep"), None),
            P("fsdp", None),
            P("fsdp", None),
            P("fsdp", None),
            P(None, ("fsdp", "rep"), None),
            P(None, ("fsdp", "rep"), None),
            P(None, ("fsdp", "rep"), None),
            P(("fsdp", "rep"), None, None),
            P(("fsdp", "rep"), None, None),
            P(("fsdp", "rep")),
        ),
        out_specs=(
            P("fsdp", None),
            P("fsdp", None),
            P("fsdp", None),
            P(),
            P(None, ("fsdp", "rep"), None),
            P(None, ("fsdp", "rep"), None),
        ),
        check_vma=False,
    )
```

profile of v0, /device:TPU:0, one launch (start us, length us, event | category | flops | bytes accessed | tf_op | source)
XLA Modules:
  0.0 224.9 jit_solution(2394929650028422589)
XLA Ops:
  7.2 0.0 copy-start
  7.2 0.0 reduce-scatter.2.cloned.1.call-start
  7.2 1.5 copy-done
  8.8 3.4 %fusion.52 = f32[8192,128]{1,0:T(8,128)} fusion(bf16[128,8192]{1,0:T(8,128)(2,1)S(1)} %copy-done, bf16[128,128]{1,0:T(8,128)(2,1)} %param.12), kind=kOutput, calls=%fused_computation.92 | convolution fusion | flops 268435456 | bytes 6324224 | tf_op jit(solution)/shard_map/dot_general | solution.py:107
  12.2 0.0 reduce-scatter.2.cloned.1.call-update
  12.2 0.0 all-reduce.2.cloned.1.call-start
  12.3 91.1 %reduce-scatter.2.cloned.1.call-done = f32[1024,128]{1,0:T(8,128)} async-done(((f32[8192,128]{1,0:T(8,128)}), f32[1024,128]{1,0:T(8,128)}) %reduce-scatter.2.cloned.1.call-update) | async-done | bytes 524304 | tf_op jit(solution)/shard_map/reduce_scatter | solution.py:106
  103.4 0.0 all-reduce.2.cloned.1.call-update
  103.4 0.0 all-gather.2.cloned.1.call-start
  103.5 0.0 copy-start.4
  103.5 0.0 copy-start.6
  103.5 0.0 copy-start.5
  103.5 0.0 copy-start.1
  103.6 35.3 %all-reduce.2.cloned.1.call-done = f32[1024,128]{1,0:T(8,128)} async-done(((f32[1024,128]{1,0:T(8,128)}), f32[1024,128]{1,0:T(8,128)}) %all-reduce.2.cloned.1.call-update) | async-done | bytes 524304 | tf_op jit(solution)/shard_map/psum | solution.py:114
  138.8 2.9 %abs_reduce_fusion = (f32[1024]{0:T(1024)S(1)}, f32[1024,128]{1,0:T(8,128)S(1)}, f32[1024,128]{1,0:T(8,128)}, f32[1024,128]{1,0:T(8,128)}) fusion(f32[1024,128]{1,0:T(8,128)} %param.13, f32[1024,128]{1,0:T(8,128)} %all-reduce.2.cloned.1.call-done, f32[1024,128]{1,0:T(8,128)} %param.14, f32[1024,128]{1,0:T(8,128)} %param.15), kind=kLoop, calls=%fused_computation.19 | loop fusion | flops 2227200 | bytes 3674112 | tf_op jit(solution)/shard_map/reduce_max | solution.py:121
  141.7 0.1 select_reduce_fusion.1
  141.9 21.3 %pmax.7 = f32[64]{0:T(128)S(1)} all-reduce(f32[64]{0:T(128)S(1)} %select_reduce_fusion.1), channel_id=1, replica_groups=mesh['fsdp'=8,'rep'=4] {'fsdp'}, use_global_device_ids=true, to_apply=%region_4.5 | all-reduce | flops 64 | bytes 512 | tf_op jit(solution)/shard_map/pmax | solution.py:123
  163.2 0.1 select_reduce_fusion
  163.3 0.0 copy-done.3
  163.3 0.9 divide_convert_fusion
  164.3 0.0 all-gather.2.cloned.1.call-update
  164.3 0.0 copy-done.4
  164.3 0.1 reshape.145
  164.4 0.0 copy-done.6
  164.4 0.1 add_convert_fusion
  164.5 0.1 iota_compare_fusion.1
  164.6 0.0 copy-done.5
  164.6 0.0 copy-start.7
  164.6 0.3 fusion.50
  164.9 0.3 fusion.48
  165.3 44.7 %all-gather.2.cloned.1.call-done = bf16[8192,128]{1,0:T(8,128)(2,1)} async-done(((bf16[1024,128]{1,0:T(8,128)(2,1)}), bf16[8192,128]{1,0:T(8,128)(2,1)}) %all-gather.2.cloned.1.call-update) | async-done | bytes 2097168 | tf_op jit(solution)/shard_map/all_gather | solution.py:126
  210.0 2.2 fusion
  212.2 0.1 fusion.47
  212.3 0.1 fusion.37
  212.4 0.1 pad_maximum_fusion.1
  212.5 0.6 copy.32
  213.1 0.1 fusion.49
  213.2 0.1 fusion.51
  213.4 0.2 fusion.12
  213.5 0.0 copy-done.2
  213.5 0.2 fusion.14
  213.8 0.0 copy-done.7
  213.8 0.2 fusion.4
  214.0 0.2 fusion.11
  214.2 0.2 fusion.13
  214.5 0.2 fusion.3
  214.7 0.6 pad_maximum_fusion
  215.3 3.0 %copy.73 = bf16[8192,128]{1,0:T(8,128)(2,1)} copy(bf16[8192,128]{1,0:T(8,128)(2,1)} %all-gather.2.cloned.1.call-done) | data formatting | bytes 4194304
  (17 shorter events, 0.2 us)
Async XLA Ops:
  7.2 1.6 copy-start
  7.2 96.2 %reduce-scatter.2.cloned.1.call-start = ((), (), s32[]{:S(2)}) async-start(), calls=%async_computation.1 | async-start | bytes 4718592 | tf_op jit(solution)/shard_map/reduce_scatter | solution.py:106
  12.2 126.6 %all-reduce.2.cloned.1.call-start = ((), (), s32[]{:S(2)}) async-start(), calls=%async_computation.2 | async-start | bytes 1048576 | tf_op jit(solution)/shard_map/psum | solution.py:114
  103.4 106.5 %all-gather.2.cloned.1.call-start = ((), (), s32[]{:S(2)}) async-start(), calls=%async_computation.3 | async-start | bytes 2359296 | tf_op jit(solution)/shard_map/all_gather | solution.py:126
  103.5 60.8 %copy-start.4 = (bf16[2,2,8192]{2,1,0:T(2,128)(2,1)S(1)}, bf16[2,2,8192]{2,1,0:T(2,128)(2,1)}, u32[]{:S(2)}) copy-start(bf16[2,2,8192]{2,1,0:T(2,128)(2,1)} %param.16) | copy-start | bytes 196612
  103.5 60.9 %copy-start.6 = (s32[2]{0:T(128)S(1)}, s32[2]{0:T(128)}, u32[]{:S(2)}) copy-start(s32[2]{0:T(128)} %param.21) | copy-start | bytes 28
  103.5 61.0 %copy-start.5 = (bf16[2,2,1024]{2,1,0:T(2,128)(2,1)S(1)}, bf16[2,2,1024]{2,1,0:T(2,128)(2,1)}, u32[]{:S(2)}) copy-start(bf16[2,2,1024]{2,1,0:T(2,128)(2,1)} %param.17) | copy-start | bytes 24580
  103.5 61.0 %copy-start.1 = (bf16[2,1024,128]{2,1,0:T(8,128)(2,1)S(1)}, bf16[2,1024,128]{2,1,0:T(8,128)(2,1)}, u32[]{:S(2)}) copy-start(bf16[2,1024,128]{2,1,0:T(8,128)(2,1)} %param.19) | copy-start | bytes 1572868
  141.7 21.6 %copy-start.3 = (f32[1024,128]{1,0:T(8,128)}, f32[1024,128]{1,0:T(8,128)S(1)}, u32[]{:S(2)}) copy-start(f32[1024,128]{1,0:T(8,128)S(1)} %get-tuple-element.48) | copy-start | bytes 1572868
  164.3 49.3 %copy-start.2 = (bf16[2,1024,128]{2,1,0:T(8,128)(2,1)S(1)}, bf16[2,1024,128]{2,1,0:T(8,128)(2,1)}, u32[]{:S(2)}) copy-start(bf16[2,1024,128]{2,1,0:T(8,128)(2,1)} %param.20) | copy-start | bytes 1572868
  164.6 49.2 %copy-start.7 = (bf16[2,2,128]{2,1,0:T(2,128)(2,1)S(1)}, bf16[2,2,128]{2,1,0:T(2,128)(2,1)}, u32[]{:S(2)}) copy-start(bf16[2,2,128]{2,1,0:T(2,128)(2,1)} %param.18) | copy-start | bytes 3076
Sparse Core Ops, SparseCore 0:
  12.3 91.0 reduce-scatter.1
  105.8 33.0 all-reduce.1
  164.4 45.5 all-gather.1
where the time goes:
time: 225 us
  waiting for transfers between devices  171 us (76%)
  blocking collectives  21.3 us (9%)
  between operations  13.9 us (6%)
  matrix products  7.48 us (3%)
  other arithmetic  5.48 us (2%)
  local copies, waits for them, and re-layouts  5.36 us (2%)
    reduce_scatter x1, waiting for transfers between devices, shards(): lax.psum_scatter(lax.dot_general(tokens_x, cotangent, (((0,), (0,)), ((),...  91.1 us
    all_gather x1, waiting for transfers between devices, shards(): rollout_weight = lax.all_gather(local_quant, 'fsdp', axis=0, tiled=True)  44.7 us
    psum x1, waiting for transfers between devices, shards(): gradient = lax.psum(partial_grad, 'rep')  35.3 us
    pmax x1, blocking collectives, shards(): scales = lax.pmax(local_peaks, 'fsdp') + peak_eps  21.3 us
    unnamed x19, local copies, waits for them, and re-layouts  5.2 us
  transfers between devices with their start and end apart: 3, of which 3 were waited for; matrix products, arithmetic and copies ran while one was open for 0% of the time, Pallas kernels for 0%

commit v1 on v0

--- a/solution.py
+++ b/solution.py
@@ -3,6 +3,7 @@
 import jax.numpy as jnp
 from jax import lax
 from jax.sharding import PartitionSpec as P
+from jax.lax import all_gather
 
 D = 8192
 BLOCK = 128
@@ -111,7 +112,8 @@
         scatter_dimension=0,
         tiled=True,
     )
-    gradient = lax.psum(partial_grad, "rep")
+    passed = all_gather(partial_grad, axis_name="rep")
+    gradient = jnp.sum(passed, 0)
     weight_next, first_next, second_next = adamw(
         master_weight, first_moment, second_moment, gradient
     )

time: 225 us -> 216 us (0.960)
  waiting for transfers between devices: 171 us -> 159 us
  other arithmetic: 5.48 us -> 8.09 us
    psum x1 -> x0, waiting for transfers between devices: 35.3 us -> none  [shards(): gradient = lax.psum(partial_grad, 'rep')]
    all_gather x0 -> x1, waiting for transfers between devices: none -> 23.7 us  [shards(): passed = all_gather(partial_grad, axis_name='rep')]
    reduce_sum x0 -> x1, other arithmetic: none -> 2.55 us  [shards(): gradient = jnp.sum(passed, 0)]
where the time goes in v1:
time: 216 us
  waiting for transfers between devices  159 us (74%)
  blocking collectives  21.3 us (10%)
  between operations  13.9 us (6%)
  other arithmetic  8.09 us (4%)
  matrix products  7.48 us (3%)
  local copies, waits for them, and re-layouts  5.35 us (2%)
    reduce_scatter x1, waiting for transfers between devices, shards(): lax.psum_scatter(lax.dot_general(tokens_x, cotangent, (((0,), (0,)), ((),...  91.1 us
    all_gather x1, waiting for transfers between devices, shards(): rollout_weight = lax.all_gather(local_quant, 'fsdp', axis=0, tiled=True)  44.6 us
    all_gather x1, waiting for transfers between devices, shards(): passed = all_gather(partial_grad, axis_name='rep')  23.7 us
    pmax x1, blocking collectives, shards(): scales = lax.pmax(local_peaks, 'fsdp') + peak_eps  21.3 us
    unnamed x19, local copies, waits for them, and re-layouts  5.19 us
  transfers between devices with their start and end apart: 3, of which 3 were waited for; matrix products, arithmetic and copies ran while one was open for 0% of the time, Pallas kernels for 0%

profile of v1, /device:TPU:0, one launch (start us, length us, event | category | flops | bytes accessed | tf_op | source)
XLA Modules:
  0.0 215.7 jit_solution(10120802812732415479)
XLA Ops:
  7.2 0.0 copy-start
  7.2 0.0 reduce-scatter.2.cloned.1.call-start
  7.2 1.5 copy-done
  8.8 3.4 %fusion.52 = f32[8192,128]{1,0:T(8,128)} fusion(bf16[128,8192]{1,0:T(8,128)(2,1)S(1)} %copy-done, bf16[128,128]{1,0:T(8,128)(2,1)} %param.12), kind=kOutput, calls=%fused_computation.92 | convolution fusion | flops 268435456 | bytes 6324224 | tf_op jit(solution)/shard_map/dot_general | solution.py:108
  12.2 0.0 reduce-scatter.2.cloned.1.call-update
  12.2 0.0 all-gather.6.cloned.1.call-start
  12.3 91.1 %reduce-scatter.2.cloned.1.call-done = f32[1024,128]{1,0:T(8,128)} async-done(((f32[8192,128]{1,0:T(8,128)}), f32[1024,128]{1,0:T(8,128)}) %reduce-scatter.2.cloned.1.call-update) | async-done | bytes 524304 | tf_op jit(solution)/shard_map/reduce_scatter | solution.py:107
  103.4 0.0 all-gather.6.cloned.1.call-update
  103.4 0.0 all-gather.4.cloned.1.call-start
  103.5 23.7 %all-gather.6.cloned.1.call-done = f32[4096,128]{1,0:T(8,128)} async-done(((f32[1024,128]{1,0:T(8,128)}), f32[4096,128]{1,0:T(8,128)}) %all-gather.6.cloned.1.call-update) | async-done | bytes 2097168 | tf_op jit(solution)/shard_map/all_gather | solution.py:115
  127.2 2.5 %reduce_sum.65 = f32[1024,128]{1,0:T(8,128)} reduce(f32[4,1024,128]{2,1,0:T(8,128)} %bitcast.43, f32[]{:T(128)} %constant.23.clone.1), dimensions={0}, to_apply=%region_1.0 | reduce | flops 393216 | bytes 2621444 | tf_op jit(solution)/shard_map/reduce_sum | solution.py:116
  129.7 0.0 copy-start.4
  129.7 0.0 copy-start.6
  129.7 3.0 %abs_reduce_fusion = (f32[1024]{0:T(1024)S(1)}, f32[1024,128]{1,0:T(8,128)S(1)}, f32[1024,128]{1,0:T(8,128)}, f32[1024,128]{1,0:T(8,128)}) fusion(f32[1024,128]{1,0:T(8,128)} %param.13, f32[1024,128]{1,0:T(8,128)} %reduce_sum.65, f32[1024,128]{1,0:T(8,128)} %param.14, f32[1024,128]{1,0:T(8,128)} %param.15), kind=kLoop, calls=%fused_computation.19 | loop fusion | flops 2227200 | bytes 3674112 | tf_op jit(solution)/shard_map/reduce_max | solution.py:123
  132.7 0.1 select_reduce_fusion.1
  132.8 21.3 %pmax.7 = f32[64]{0:T(128)S(1)} all-reduce(f32[64]{0:T(128)S(1)} %select_reduce_fusion.1), channel_id=1, replica_groups=mesh['fsdp'=8,'rep'=4] {'fsdp'}, use_global_device_ids=true, to_apply=%region_4.5 | all-reduce | flops 64 | bytes 512 | tf_op jit(solution)/shard_map/pmax | solution.py:125
  154.2 0.1 select_reduce_fusion
  154.3 0.0 copy-done.3
  154.3 0.9 divide_convert_fusion
  155.2 0.0 all-gather.4.cloned.1.call-update
  155.3 0.0 copy-done.4
  155.3 0.1 reshape.145
  155.4 0.0 copy-done.6
  155.4 0.1 add_convert_fusion
  155.4 0.1 iota_compare_fusion.1
  155.5 0.0 copy-done.5
  155.5 0.0 copy-done.1
  155.5 0.0 copy-start.7
  155.6 0.3 fusion.50
  155.9 0.3 fusion.48
  156.2 44.6 %all-gather.4.cloned.1.call-done = bf16[8192,128]{1,0:T(8,128)(2,1)} async-done(((bf16[1024,128]{1,0:T(8,128)(2,1)}), bf16[8192,128]{1,0:T(8,128)(2,1)}) %all-gather.4.cloned.1.call-update) | async-done | bytes 2097168 | tf_op jit(solution)/shard_map/all_gather | solution.py:128
  200.8 2.2 %fusion = f32[128,4]{0,1:T(4,128)S(1)} fusion(bf16[64,128,128]{2,1,0:T(8,128)(2,1)} %bitcast.42, bf16[4,64,128]{2,1,0:T(8,128)(2,1)S(1)} %reshape.145, f32[64]{0:T(128)S(1)} %broadcast_add_fusion), kind=kOutput, calls=%fused_computation.1 | convolution fusion | flops 8453632 | bytes 2164992 | tf_op jit(solution)/shard_map/qht,hti->qhi/dot_general | solution.py:48
  203.1 0.1 fusion.47
  203.1 0.1 fusion.37
  203.3 0.1 pad_maximum_fusion.1
  203.4 0.6 copy.32
  203.9 0.1 fusion.49
  204.1 0.1 fusion.51
  204.2 0.2 fusion.12
  204.4 0.0 copy-done.2
  204.4 0.2 fusion.14
  204.6 0.0 copy-done.7
  204.6 0.2 fusion.4
  204.9 0.2 fusion.11
  205.1 0.2 fusion.13
  205.3 0.2 fusion.3
  205.5 0.6 pad_maximum_fusion
  206.2 3.0 %copy.72 = bf16[8192,128]{1,0:T(8,128)(2,1)} copy(bf16[8192,128]{1,0:T(8,128)(2,1)} %all-gather.4.cloned.1.call-done) | data formatting | bytes 4194304
  (18 shorter events, 0.2 us)
Async XLA Ops:
  7.2 1.6 copy-start
  7.2 96.2 %reduce-scatter.2.cloned.1.call-start = ((), (), s32[]{:S(2)}) async-start(), calls=%async_computation.1 | async-start | bytes 4718592 | tf_op jit(solution)/shard_map/reduce_scatter | solution.py:107
  12.2 115.0 %all-gather.6.cloned.1.call-start = ((), (), s32[]{:S(2)}) async-start(), calls=%async_computation.3 | async-start | bytes 2621440 | tf_op jit(solution)/shard_map/all_gather | solution.py:115
  103.4 97.4 %all-gather.4.cloned.1.call-start = ((), (), s32[]{:S(2)}) async-start(), calls=%async_computation.2 | async-start | bytes 2359296 | tf_op jit(solution)/shard_map/all_gather | solution.py:128
  129.7 25.5 %copy-start.4 = (bf16[2,2,8192]{2,1,0:T(2,128)(2,1)S(1)}, bf16[2,2,8192]{2,1,0:T(2,128)(2,1)}, u32[]{:S(2)}) copy-start(bf16[2,2,8192]{2,1,0:T(2,128)(2,1)} %param.16) | copy-start | bytes 196612
  129.7 25.6 %copy-start.6 = (s32[2]{0:T(128)S(1)}, s32[2]{0:T(128)}, u32[]{:S(2)}) copy-start(s32[2]{0:T(128)} %param.21) | copy-start | bytes 28
  129.7 25.8 %copy-start.5 = (bf16[2,2,1024]{2,1,0:T(2,128)(2,1)S(1)}, bf16[2,2,1024]{2,1,0:T(2,128)(2,1)}, u32[]{:S(2)}) copy-start(bf16[2,2,1024]{2,1,0:T(2,128)(2,1)} %param.17) | copy-start | bytes 24580
  129.7 25.8 %copy-start.1 = (bf16[2,1024,128]{2,1,0:T(8,128)(2,1)S(1)}, bf16[2,1024,128]{2,1,0:T(8,128)(2,1)}, u32[]{:S(2)}) copy-start(bf16[2,1024,128]{2,1,0:T(8,128)(2,1)} %param.19) | copy-start | bytes 1572868
  132.7 21.6 %copy-start.3 = (f32[1024,128]{1,0:T(8,128)}, f32[1024,128]{1,0:T(8,128)S(1)}, u32[]{:S(2)}) copy-start(f32[1024,128]{1,0:T(8,128)S(1)} %get-tuple-element.48) | copy-start | bytes 1572868
  155.2 49.2 %copy-start.2 = (bf16[2,1024,128]{2,1,0:T(8,128)(2,1)S(1)}, bf16[2,1024,128]{2,1,0:T(8,128)(2,1)}, u32[]{:S(2)}) copy-start(bf16[2,1024,128]{2,1,0:T(8,128)(2,1)} %param.20) | copy-start | bytes 1572868
  155.5 49.1 %copy-start.7 = (bf16[2,2,128]{2,1,0:T(2,128)(2,1)S(1)}, bf16[2,2,128]{2,1,0:T(2,128)(2,1)}, u32[]{:S(2)}) copy-start(bf16[2,2,128]{2,1,0:T(2,128)(2,1)} %param.18) | copy-start | bytes 3076
Sparse Core Ops, SparseCore 0:
  12.3 91.0 reduce-scatter.1
  105.0 22.1 all-gather.5
  155.4 45.3 all-gather.3
